TPU v7x, 32 devices: a whole 2x2x4 slice. The times are simulated.
32 devices in a mesh: clips: 2 (over x), ulysses: 4 (over y, core), tm: 4 (over z).
Axes of the slice: x: 2, y: 2, z: 4, core: 2. Of those that a mesh axis runs over, the one named last changes fastest.
Arguments:
- queries: bfloat16 [4096, 3072], P(('clips', 'tm', 'ulysses')), parts along dimension 0, may hold values from -90 to 90
- key_vectors: bfloat16 [4096, 3072], P(('clips', 'tm', 'ulysses')), parts along dimension 0, may hold values from -5 to 5
- value_vectors: bfloat16 [4096, 3072], P(('clips', 'tm', 'ulysses')), parts along dimension 0, may hold values from -6 to 6
- grad_out: bfloat16 [4096, 3072], P(('clips', 'tm', 'ulysses')), parts along dimension 0, may hold values from -6 to 6
- key_tiles: int32 [64, 3], P('clips'), parts along dimension 0, may hold values from 0 to 31, as said below
- tile_counts: int32 [64], P('clips'), parts along dimension 0, may hold values from 2 to 3, as said below
Outputs:
- attended: bfloat16 [4096, 3072], P(('clips', 'tm', 'ulysses')), parts along dimension 0
- grad_queries: bfloat16 [4096, 3072], P(('clips', 'tm', 'ulysses')), parts along dimension 0
- grad_keys: bfloat16 [4096, 3072], P(('clips', 'tm', 'ulysses')), parts along dimension 0
- grad_values: bfloat16 [4096, 3072], P(('clips', 'tm', 'ulysses')), parts along dimension 0
There are 2 independent parts, one for each index of `clips`. A program takes and returns all parts, laid end to end along the dimension named above; each array names one. Nothing has to cross between parts.
Inputs may be any that keep to these rules, and one draw needn't show every extreme that they name: `key_tiles`: row i holds distinct tiles of the frame of query tile i and of the frames just before and after it; entry 0 is tile i itself, then one tile of the frame before and one of the frame after where those frames exist, then the rest in no fixed order; entries from position tile_counts[i] on repeat entry 0. The query tiles of one frame together list exactly 1 tiles of the frame before it and exactly 1 of the frame after it, where those frames exist. `tile_counts`: the first 1 query tiles of every frame have count 3.
All inputs are finite; a program needn't handle non-finite values.
Results may differ from a plain program's by a relative error of at most 0.022.
Values may be sent and summed in bfloat16 or wider, within the bound.
A program may use at most 192 MiB of HBM per device.

v0:
```python
import functools

import jax
import jax.numpy as jnp
from jax import lax
from jax.experimental import pallas as pl
from jax.experimental.pallas import tpu as pltpu
from jax.sharding import PartitionSpec as P

HEAD_DIM = 64
TILE = 64
FRAMES_SLAB = 2
LANES = 128
DEAD = -1e30
BLOCK_LIMIT = 384 * 512
CHUNK_HEADS = 6
MESH = pl.DeviceIdType.MESH
BF16 = jnp.bfloat16
F32 = jnp.float32


def position(group):
    place = lax.axis_index("ulysses")
    frame = lax.axis_index("tm") * FRAMES_SLAB + place // group
    return frame, place % group, place - place % group


def frame_device(frame, group, member):
    return {
        "tm": frame // FRAMES_SLAB,
        "ulysses": (frame % FRAMES_SLAB) * group + member,
    }


def greet(group, frames):
    frame, member, base = position(group)
    barrier = pltpu.get_barrier_semaphore()
    for step in range(1, group):
        peer = base + (member + step) % group
        pl.semaphore_signal(barrier, inc=1, device_id={"ulysses": peer}, device_id_type=MESH)

    neighbours = ((frame > 0, -1), (frame < frames - 1, 1))
    for exists, step in neighbours:
        @pl.when(exists)
        def _():
            pl.semaphore_signal(
                barrier, inc=1, device_id=frame_device(frame + step, group, member),
                device_id_type=MESH,
            )

    near = jnp.where(frame > 0, 1, 0) + jnp.where(frame < frames - 1, 1, 0)
    pl.semaphore_wait(barrier, group - 1 + near)


def remote(source, target, send, receive, device):
    return pltpu.make_async_remote_copy(
        src_ref=source, dst_ref=target, send_sem=send, recv_sem=receive,
        device_id=device, device_id_type=MESH,
    )


def heads_math(query, grad, keys, values, bias):
    scale = HEAD_DIM ** (-0.5)
    lanes = lax.broadcasted_iota(jnp.int32, query.shape, 1)
    first = lanes < HEAD_DIM
    nothing = jnp.zeros_like(query)
    query = query * jnp.asarray(scale, BF16)
    queries = jnp.concatenate([jnp.where(first, query, nothing), jnp.where(first, nothing, query)])
    grads = jnp.concatenate([jnp.where(first, grad, nothing), jnp.where(first, nothing, grad)])
    rows, columns = keys.shape[0], queries.shape[0]

    def dot(left, right, dims):
        return lax.dot_general(left, right, (dims, ((), ())), preferred_element_type=F32)

    def pick(both):
        return jnp.where(first, both[: columns // 2], both[columns // 2 :])

    scores = dot(keys, queries, ((1,), (1,)))
    bias = jnp.concatenate([bias, bias], axis=1)
    scores = scores.reshape(rows // TILE, TILE, columns) + bias[:, None, :]
    scores = scores.reshape(rows, columns)
    expo = jnp.exp(scores - jnp.max(scores, axis=0, keepdims=True))
    probs = expo * (1.0 / jnp.sum(expo, axis=0, keepdims=True))
    probs_low = probs.astype(BF16)
    grad_probs = dot(values, grads, ((1,), (1,)))
    delta = jnp.sum(probs * grad_probs, axis=0, keepdims=True)
    grad_low = (probs * (grad_probs - delta)).astype(BF16)
    attended = pick(dot(probs_low, values, ((0,), (0,)))).astype(BF16)
    grad_query = (pick(dot(grad_low, keys, ((0,), (0,)))) * scale).astype(BF16)
    key_part = dot(grad_low, queries, ((1,), (0,)))
    value_part = dot(probs_low, grads, ((1,), (0,)))
    return attended, grad_query, key_part, value_part


def block_rows(frame_rows, ext_rows):
    tiles = frame_rows // TILE
    for step in range(tiles, 0, -1):
        if tiles % step == 0 and 2 * step * TILE * ext_rows <= BLOCK_LIMIT:
            return step * TILE
    return TILE


def listing(tiles, counts, reader, source, frame_tiles, frames):
    reader = jnp.clip(reader, 0, frames - 1)
    masks = []
    for row in range(frame_tiles):
        tile = reader * frame_tiles + row
        mask = jnp.int32(0)
        for slot in range(tiles.shape[0]):
            inside = tiles[slot, tile] - source * frame_tiles
            good = (inside >= 0) & (inside < frame_tiles) & (slot < counts[tile])
            bit = lax.shift_left(jnp.int32(1), jnp.clip(inside, 0, frame_tiles - 1))
            mask = mask | jnp.where(good, bit, 0)
        masks.append(mask)
    return masks


def nth_tiles(masks, frame_tiles, count):
    union = functools.reduce(lambda left, right: left | right, masks)
    seen = jnp.int32(0)
    picked = [[] for _ in range(count)]
    for tile in range(frame_tiles):
        bit = (union >> tile) & 1
        for spot in range(count):
            picked[spot].append((bit == 1) & (seen == spot))
        seen = seen + bit
    return picked


def fused_kernel(
    group, frames, count, chunks, tiles, counts, q_in, k_in, v_in, g_in,
    out_a, out_q, out_k, out_v,
    ext, own, bias, stage, parts, result, border, landed,
    send, recv, near, halo_send, halo_recv,
    back_send, back_recv, out_send, out_recv, out_near,
):
    frame, member, base = position(group)
    rows = q_in.shape[0]
    frame_rows, chunk_width = own.shape[2], own.shape[3]
    width = chunk_width * chunks
    edge = count * TILE
    frame_tiles = frame_rows // TILE
    has_low, has_high = frame > 0, frame < frames - 1

    def lanes_of(which, chunk):
        return pl.ds(pl.multiple_of(which * width + chunk * chunk_width, LANES), chunk_width)

    def rows_of(which, start=0):
        return pl.ds(pl.multiple_of(which * rows + start, TILE), rows)

    sources = (k_in, v_in, q_in, g_in)

    def landing(number, chunk):
        if number < 2:
            return ext.at[number, chunk, rows_of(member, edge)]
        return own.at[number - 2, chunk, rows_of(member)]

    order = [(number, chunk) for chunk in range(chunks) for number in (0, 1)]
    order += [(number, chunk) for chunk in range(chunks) for number in (2, 3)]
    arriving = {}
    for number, chunk in order:
        copy = pltpu.make_async_copy(
            sources[number].at[:, lanes_of(member, chunk)], landing(number, chunk),
            near.at[number, chunk],
        )
        copy.start()
        arriving[number, chunk] = [copy]
    greet(group, frames)
    for number, chunk in order:
        for step in range(1, group):
            peer = (member + step) % group
            copy = remote(
                sources[number].at[:, lanes_of(peer, chunk)], landing(number, chunk),
                send.at[number, chunk, step - 1], recv.at[number, chunk, step - 1],
                {"ulysses": base + peer},
            )
            copy.start()
            arriving[number, chunk].append(copy)

    up_picks = nth_tiles(
        listing(tiles, counts, frame + 1, frame, frame_tiles, frames), frame_tiles, count
    )
    down_picks = nth_tiles(
        listing(tiles, counts, frame - 1, frame, frame_tiles, frames), frame_tiles, count
    )
    picks = (up_picks, down_picks)

    halo_rows = (pl.ds(0, edge), pl.ds(edge + frame_rows, edge))

    def halo_copy(number, way, chunk, target):
        return remote(
            stage.at[number, way, chunk], ext.at[number, chunk, halo_rows[way]],
            halo_send.at[number, way, chunk], halo_recv.at[number, way, chunk],
            frame_device(target, group, member),
        )

    def back_copy(number, way, chunk, target):
        return remote(
            border.at[number, way, chunk], landed.at[number, way, chunk],
            back_send.at[number, way, chunk], back_recv.at[number, way, chunk],
            frame_device(target, group, member),
        )

    for way, exists in enumerate((has_low, has_high)):
        @pl.when(jnp.logical_not(exists))
        def _():
            for number in range(2):
                for chunk in range(chunks):
                    ext[number, chunk, halo_rows[way]] = jnp.zeros((edge, chunk_width), BF16)
                    landed[number, 1 - way, chunk] = jnp.zeros((edge, chunk_width), BF16)

    for chunk in range(chunks):
        for number in range(2):
            for copy in arriving[number, chunk]:
                copy.wait()
            for way in range(2):
                for spot in range(count):
                    chosen = ext[number, chunk, pl.ds(edge, TILE)]
                    for tile in range(1, frame_tiles):
                        here = ext[number, chunk, pl.ds(edge + tile * TILE, TILE)]
                        chosen = jnp.where(picks[way][spot][tile], here, chosen)
                    stage[number, way, chunk, pl.ds(spot * TILE, TILE)] = chosen
        for way, exists in enumerate((has_high, has_low)):
            @pl.when(exists)
            def _():
                for number in range(2):
                    halo_copy(number, way, chunk, frame + (1 if way == 0 else -1)).start()

    blocks, step_rows = bias.shape[0], bias.shape[2]
    low_rows = listing(tiles, counts, frame, frame - 1, frame_tiles, frames)
    own_masks = listing(tiles, counts, frame, frame, frame_tiles, frames)
    high_rows = listing(tiles, counts, frame, frame + 1, frame_tiles, frames)

    def edge_hits(masks):
        picked = nth_tiles(masks, frame_tiles, count)
        hits = []
        for spot in range(count):
            bit = jnp.int32(0)
            for tile in range(frame_tiles):
                bit = bit + jnp.where(picked[spot][tile], 1 << tile, 0)
            hits.append([(mask & bit) != 0 for mask in masks])
        return hits

    hits = edge_hits(low_rows)
    hits += [[((mask >> tile) & 1) == 1 for mask in own_masks] for tile in range(frame_tiles)]
    hits += edge_hits(high_rows)
    block_tiles = step_rows // TILE
    inner = lax.broadcasted_iota(jnp.int32, (1, step_rows), 1) // TILE
    for number, row in enumerate(hits):
        for block in range(blocks):
            line = jnp.full((1, step_rows), DEAD, F32)
            for spot in range(block_tiles):
                level = jnp.where(row[block * block_tiles + spot], 0.0, DEAD)
                line = jnp.where(inner == spot, level, line)
            bias[block, pl.ds(number, 1)] = line

    leaving = []

    def share(number, chunk):
        target = (out_a, out_q, out_k, out_v)[number]
        columns = lanes_of(member, chunk)
        copy = pltpu.make_async_copy(
            result.at[number, chunk, rows_of(member)], target.at[:, columns],
            out_near.at[number, chunk],
        )
        copy.start()
        leaving.append(copy)
        for step in range(1, group):
            peer = (member + step) % group
            copy = remote(
                result.at[number, chunk, rows_of(peer)], target.at[:, columns],
                out_send.at[number, chunk, step - 1], out_recv.at[number, chunk, step - 1],
                {"ulysses": base + peer},
            )
            copy.start()
            leaving.append(copy)

    for chunk in range(chunks):
        for number in (2, 3):
            for copy in arriving[number, chunk]:
                copy.wait()
        for way, comes in enumerate((has_low, has_high)):
            @pl.when(comes)
            def _():
                for number in range(2):
                    halo_copy(number, way, chunk, frame).wait_recv()

        @pl.loop(0, chunk_width // LANES)
        def _(pair):
            lanes = pl.ds(pl.multiple_of(pair * LANES, LANES), LANES)
            for block in range(blocks):
                span = pl.ds(block * step_rows, step_rows)
                out, grad_rows, key_part, value_part = heads_math(
                    own[0, chunk, span, lanes], own[1, chunk, span, lanes],
                    ext[0, chunk, :, lanes], ext[1, chunk, :, lanes], bias[block],
                )
                result[0, chunk, span, lanes] = out
                result[1, chunk, span, lanes] = grad_rows
                for number, part in enumerate((key_part, value_part)):
                    if block:
                        part = part + parts[number, chunk, :, lanes]
                    parts[number, chunk, :, lanes] = part

        for number in range(2):
            for way in range(2):
                border[number, way, chunk] = parts[number, chunk, halo_rows[way]].astype(BF16)
        for way, goes in enumerate((has_low, has_high)):
            @pl.when(goes)
            def _():
                for number in range(2):
                    back_copy(number, way, chunk, frame + (1 if way else -1)).start()
        share(0, chunk)
        share(1, chunk)

    for chunk in range(chunks):
        for way, comes in enumerate((has_high, has_low)):
            @pl.when(comes)
            def _():
                for number in range(2):
                    back_copy(number, way, chunk, frame).wait_recv()
        for number in range(2):
            for tile in range(frame_tiles):
                total = parts[number, chunk, pl.ds(edge + tile * TILE, TILE)]
                for way in range(2):
                    for spot in range(count):
                        part = landed[number, way, chunk, pl.ds(spot * TILE, TILE)].astype(F32)
                        total = total + jnp.where(picks[way][spot][tile], part, 0.0)
                result[2 + number, chunk, pl.ds(tile * TILE, TILE)] = total.astype(BF16)
            share(2 + number, chunk)

    for way, (halo_goes, back_goes) in enumerate(((has_high, has_low), (has_low, has_high))):
        @pl.when(halo_goes)
        def _():
            for chunk in range(chunks):
                for number in range(2):
                    halo_copy(number, way, chunk, frame).wait_send()

        @pl.when(back_goes)
        def _():
            for chunk in range(chunks):
                for number in range(2):
                    back_copy(number, way, chunk, frame).wait_send()
    for copy in leaving:
        copy.wait()


def flush_kernel(*refs):
    held, sems = refs[8:]
    half = held.shape[1] // 2
    pieces = []
    for part in range(2):
        span = pl.ds(part * half, half)
        for number in range(4):
            slot = held.at[number, span]
            pieces.append((
                pltpu.make_async_copy(refs[number].at[span], slot, sems.at[0, number, part]),
                pltpu.make_async_copy(slot, refs[4 + number].at[span], sems.at[1, number, part]),
            ))
    for take, _ in pieces:
        take.start()
    for take, put in pieces:
        take.wait()
        put.start()
    for _, put in pieces:
        put.wait()


def per_device(frames, group, queries, key_vectors, value_vectors, grad_out, key_tiles, tile_counts):
    rows, columns = queries.shape
    width = columns // group
    frame_rows = rows * group
    frame_tiles = frame_rows // TILE
    count = max(1, frame_tiles // 8)
    edge = count * TILE
    ext_rows = frame_rows + 2 * edge
    chunk_width = CHUNK_HEADS * HEAD_DIM
    if width % chunk_width:
        chunk_width = LANES
    chunks = width // chunk_width
    step_rows = block_rows(frame_rows, ext_rows)

    smem = pl.BlockSpec(memory_space=pltpu.SMEM)
    anywhere = pl.BlockSpec(memory_space=pl.ANY)
    dma = pltpu.SemaphoreType.DMA
    own_shape = jax.ShapeDtypeStruct((rows, columns), BF16)
    results = pl.pallas_call(
        functools.partial(fused_kernel, group, frames, count, chunks),
        out_shape=(own_shape,) * 4,
        in_specs=[smem, smem] + [anywhere] * 4,
        out_specs=(anywhere,) * 4,
        scratch_shapes=[
            pltpu.VMEM((2, chunks, ext_rows, chunk_width), BF16),
            pltpu.VMEM((2, chunks, frame_rows, chunk_width), BF16),
            pltpu.VMEM((frame_rows // step_rows, ext_rows // TILE, step_rows), F32),
            pltpu.VMEM((2, 2, chunks, edge, chunk_width), BF16),
            pltpu.VMEM((2, chunks, ext_rows, chunk_width), F32),
            pltpu.VMEM((4, chunks, frame_rows, chunk_width), BF16),
            pltpu.VMEM((2, 2, chunks, edge, chunk_width), BF16),
            pltpu.VMEM((2, 2, chunks, edge, chunk_width), BF16),
            dma((4, chunks, group - 1)), dma((4, chunks, group - 1)), dma((4, chunks)),
            dma((2, 2, chunks)), dma((2, 2, chunks)), dma((2, 2, chunks)), dma((2, 2, chunks)),
            dma((4, chunks, group - 1)), dma((4, chunks, group - 1)), dma((4, chunks)),
        ],
        compiler_params=pltpu.CompilerParams(collective_id=0, has_side_effects=True),
        name="frame_attention",
    )(key_tiles.T, tile_counts, queries, key_vectors, value_vectors, grad_out)
    return pl.pallas_call(
        flush_kernel,
        out_shape=(own_shape,) * 4,
        in_specs=[anywhere] * 4,
        out_specs=(anywhere,) * 4,
        scratch_shapes=[pltpu.VMEM((4, rows, columns), BF16), dma((2, 4, 2))],
        name="flush_results",
    )(*results)


def solution(mesh):
    tokens = P(("clips", "tm", "ulysses"), None)
    group = mesh.shape["ulysses"] // FRAMES_SLAB
    frames = mesh.shape["tm"] * FRAMES_SLAB
    return jax.shard_map(
        functools.partial(per_device, frames, group),
        mesh=mesh,
        in_specs=(tokens, tokens, tokens, tokens, P("clips", None), P("clips")),
        out_specs=(tokens,) * 4,
        check_vma=False,
    )
```

profile of v0, /device:TPU:9, one launch (start us, length us, event | category | flops | bytes accessed | tf_op | source)
XLA Modules:
  0.0 46.6 jit_solution(15163185909902882358)
XLA Ops:
  0.6 43.2 %frame_attention.1 = (bf16[128,3072]{1,0:T(8,128)(2,1)}, bf16[128,3072]{1,0:T(8,128)(2,1)}, bf16[128,3072]{1,0:T(8,128)(2,1)}, bf16[128,3072]{1,0:T(8,128)(2,1)}) custom-call(s32[3,32]{1,0:T(4,128)} %bitcast.1, s32[32]{0:T(128)} %counts.1, bf16[128,3072]{1,0:T(8,128)(2,1)} %q_in.1, bf16[128,3072]{1,0:T(8,128)(2,1)} %k_in.1, bf16[128,3072]{1,0:T(8,128)(2,1)} %v_in.1, ...), custom_call_target="tpu_custom_call" | custom-call | tf_op jit(solution)/shard_map/frame_attention/pallas_call | solution.py:386
  43.8 2.8 %flush_results.1 = (bf16[128,3072]{1,0:T(8,128)(2,1)}, bf16[128,3072]{1,0:T(8,128)(2,1)}, bf16[128,3072]{1,0:T(8,128)(2,1)}, bf16[128,3072]{1,0:T(8,128)(2,1)}) custom-call(bf16[128,3072]{1,0:T(8,128)(2,1)} %get-tuple-element.8.refs_0_, bf16[128,3072]{1,0:T(8,128)(2,1)} %get-tuple-element.9.refs_1_, bf16[128,3072]{1,0:T(8,128)(2,1)} %get-tuple-element.10.refs_2_, ...), custom_call_target="tpu_custom_call" | custom-call | tf_op jit(solution)/shard_map/flush_results/pallas_call | solution.py:407
where the time goes:
time: 46.8 us; the launch traced here: 46.6 us
  Pallas kernels  46 us (98%)
  between operations  0.64 us (1%)
    pallas_call x1, Pallas kernels, per_device(): pl.pallas_call(functools.partial(fused_kernel, group, frames, count, chun...  43.2 us
    pallas_call x1, Pallas kernels, per_device(): pl.pallas_call(flush_kernel, out_shape=(own_shape,) * 4, in_specs=[anywhe...  2.79 us

commit v1 on v0

--- a/solution.py
+++ b/solution.py
@@ -345,24 +345,12 @@
 
 
 def flush_kernel(*refs):
-    held, sems = refs[8:]
-    half = held.shape[1] // 2
-    pieces = []
-    for part in range(2):
-        span = pl.ds(part * half, half)
-        for number in range(4):
-            slot = held.at[number, span]
-            pieces.append((
-                pltpu.make_async_copy(refs[number].at[span], slot, sems.at[0, number, part]),
-                pltpu.make_async_copy(slot, refs[4 + number].at[span], sems.at[1, number, part]),
-            ))
-    for take, _ in pieces:
-        take.start()
-    for take, put in pieces:
-        take.wait()
-        put.start()
-    for _, put in pieces:
-        put.wait()
+    sems = refs[8]
+    copies = [pltpu.make_async_copy(refs[n], refs[4 + n], sems.at[n]) for n in range(4)]
+    for copy in copies:
+        copy.start()
+    for copy in copies:
+        copy.wait()
 
 
 def per_device(frames, group, queries, key_vectors, value_vectors, grad_out, key_tiles, tile_counts):
@@ -380,14 +368,19 @@
     step_rows = block_rows(frame_rows, ext_rows)
 
     smem = pl.BlockSpec(memory_space=pltpu.SMEM)
-    anywhere = pl.BlockSpec(memory_space=pl.ANY)
+    vmem = pl.BlockSpec(memory_space=pltpu.VMEM)
+    hbm = pl.BlockSpec(memory_space=pltpu.HBM)
     dma = pltpu.SemaphoreType.DMA
     own_shape = jax.ShapeDtypeStruct((rows, columns), BF16)
+    arguments = [
+        pltpu.with_memory_space_constraint(value, pltpu.HBM)
+        for value in (key_tiles.T, tile_counts, queries, key_vectors, value_vectors, grad_out)
+    ]
     results = pl.pallas_call(
         functools.partial(fused_kernel, group, frames, count, chunks),
         out_shape=(own_shape,) * 4,
-        in_specs=[smem, smem] + [anywhere] * 4,
-        out_specs=(anywhere,) * 4,
+        in_specs=[smem, smem] + [hbm] * 4,
+        out_specs=(vmem,) * 4,
         scratch_shapes=[
             pltpu.VMEM((2, chunks, ext_rows, chunk_width), BF16),
             pltpu.VMEM((2, chunks, frame_rows, chunk_width), BF16),
@@ -401,15 +394,18 @@
             dma((2, 2, chunks)), dma((2, 2, chunks)), dma((2, 2, chunks)), dma((2, 2, chunks)),
             dma((4, chunks, group - 1)), dma((4, chunks, group - 1)), dma((4, chunks)),
         ],
-        compiler_params=pltpu.CompilerParams(collective_id=0, has_side_effects=True),
+        compiler_params=pltpu.CompilerParams(
+            collective_id=0, has_side_effects=True, vmem_limit_bytes=32 << 20
+        ),
         name="frame_attention",
-    )(key_tiles.T, tile_counts, queries, key_vectors, value_vectors, grad_out)
+    )(*arguments)
     return pl.pallas_call(
         flush_kernel,
         out_shape=(own_shape,) * 4,
-        in_specs=[anywhere] * 4,
-        out_specs=(anywhere,) * 4,
-        scratch_shapes=[pltpu.VMEM((4, rows, columns), BF16), dma((2, 4, 2))],
+        in_specs=[vmem] * 4,
+        out_specs=(hbm,) * 4,
+        scratch_shapes=[dma((4,))],
+        compiler_params=pltpu.CompilerParams(vmem_limit_bytes=16 << 20),
         name="flush_results",
     )(*results)
 

time: 46.8 us -> 45.6 us (0.974)
  Pallas kernels: 46 us -> 44.8 us
    pallas_call x1, Pallas kernels: 2.79 us -> 1.69 us  [per_device(): pl.pallas_call(flush_kernel, out_shape=(own_shape,) * 4, in_specs=[vmem]...]
where the time goes in v1:
time: 45.6 us; the launch traced here: 45.4 us
  Pallas kernels  44.8 us (98%)
  between operations  0.64 us (1%)
    pallas_call x1, Pallas kernels, per_device(): pl.pallas_call(functools.partial(fused_kernel, group, frames, count, chun...  43.1 us
    pallas_call x1, Pallas kernels, per_device(): pl.pallas_call(flush_kernel, out_shape=(own_shape,) * 4, in_specs=[vmem]...  1.69 us

profile of v1, /device:TPU:9, one launch (start us, length us, event | category | flops | bytes accessed | tf_op | source)
XLA Modules:
  0.0 45.4 jit_solution(5547333661932599469)
XLA Ops:
  0.6 43.1 %frame_attention.1 = (bf16[128,3072]{1,0:T(8,128)(2,1)S(1)}, bf16[128,3072]{1,0:T(8,128)(2,1)S(1)}, bf16[128,3072]{1,0:T(8,128)(2,1)S(1)}, bf16[128,3072]{1,0:T(8,128)(2,1)S(1)}) custom-call(s32[3,32]{1,0:T(4,128)} %bitcast.1, s32[32]{0:T(128)} %counts.1, bf16[128,3072]{1,0:T(8,128)(2,1)} %q_in.1, bf16[128,3072]{1,0:T(8,128)(2,1)} %k_in.1, ...), custom_call_target="tpu_custom_call" | custom-call | tf_op jit(solution)/shard_map/frame_attention/pallas_call | solution.py:379
  43.7 1.7 %flush_results.1 = (bf16[128,3072]{1,0:T(8,128)(2,1)}, bf16[128,3072]{1,0:T(8,128)(2,1)}, bf16[128,3072]{1,0:T(8,128)(2,1)}, bf16[128,3072]{1,0:T(8,128)(2,1)}) custom-call(bf16[128,3072]{1,0:T(8,128)(2,1)S(1)} %get-tuple-element.8.refs_0_, bf16[128,3072]{1,0:T(8,128)(2,1)S(1)} %get-tuple-element.9.refs_1_, bf16[128,3072]{1,0:T(8,128)(2,1)S(1)} %get-tuple-element.10.refs_2_, ...), custom_call_target="tpu_custom_call" | custom-call | tf_op jit(solution)/shard_map/flush_results/pallas_call | solution.py:402

commit v2 on v1

v2 whole, which is shorter than its diff:
```python
import functools

import jax
import jax.numpy as jnp
from jax import lax
from jax.experimental import pallas as pl
from jax.experimental.pallas import tpu as pltpu
from jax.sharding import PartitionSpec as P

HEAD_DIM = 64
TILE = 64
FRAMES_SLAB = 2
LANES = 128
DEAD = -1e30
BLOCK_LIMIT = 384 * 512
CHUNK = 256
LAG = 1
MESH = pl.DeviceIdType.MESH
BF16 = jnp.bfloat16
F32 = jnp.float32


def remote(source, target, send, receive, device):
    return pltpu.make_async_remote_copy(
        src_ref=source, dst_ref=target, send_sem=send, recv_sem=receive,
        device_id=device, device_id_type=MESH,
    )


def heads_math(query, grad, keys, values, bias):
    scale = HEAD_DIM ** (-0.5)
    lanes = lax.broadcasted_iota(jnp.int32, query.shape, 1)
    first = lanes < HEAD_DIM
    nothing = jnp.zeros_like(query)
    query = query * jnp.asarray(scale, BF16)
    queries = jnp.concatenate([jnp.where(first, query, nothing), jnp.where(first, nothing, query)])
    grads = jnp.concatenate([jnp.where(first, grad, nothing), jnp.where(first, nothing, grad)])
    rows, columns = keys.shape[0], queries.shape[0]

    def dot(left, right, dims):
        return lax.dot_general(left, right, (dims, ((), ())), preferred_element_type=F32)

    def pick(both):
        return jnp.where(first, both[: columns // 2], both[columns // 2 :])

    scores = dot(keys, queries, ((1,), (1,)))
    bias = jnp.concatenate([bias, bias], axis=1)
    scores = scores.reshape(rows // TILE, TILE, columns) + bias[:, None, :]
    scores = scores.reshape(rows, columns)
    expo = jnp.exp(scores - jnp.max(scores, axis=0, keepdims=True))
    probs = expo * (1.0 / jnp.sum(expo, axis=0, keepdims=True))
    probs_low = probs.astype(BF16)
    grad_probs = dot(values, grads, ((1,), (1,)))
    delta = jnp.sum(probs * grad_probs, axis=0, keepdims=True)
    grad_low = (probs * (grad_probs - delta)).astype(BF16)
    attended = pick(dot(probs_low, values, ((0,), (0,)))).astype(BF16)
    grad_query = (pick(dot(grad_low, keys, ((0,), (0,)))) * scale).astype(BF16)
    key_part = dot(grad_low, queries, ((1,), (0,)))
    value_part = dot(probs_low, grads, ((1,), (0,)))
    return attended, grad_query, key_part, value_part


def block_rows(frame_rows, ext_rows):
    tiles = frame_rows // TILE
    for step in range(tiles, 0, -1):
        if tiles % step == 0 and 2 * step * TILE * ext_rows <= BLOCK_LIMIT:
            return step * TILE
    return TILE


def listing(tiles, counts, reader, source, frame_tiles, frames):
    reader = jnp.clip(reader, 0, frames - 1)
    masks = []
    for row in range(frame_tiles):
        tile = reader * frame_tiles + row
        mask = jnp.int32(0)
        for slot in range(tiles.shape[0]):
            inside = tiles[slot, tile] - source * frame_tiles
            good = (inside >= 0) & (inside < frame_tiles) & (slot < counts[tile])
            bit = lax.shift_left(jnp.int32(1), jnp.clip(inside, 0, frame_tiles - 1))
            mask = mask | jnp.where(good, bit, 0)
        masks.append(mask)
    return masks


def nth_tiles(masks, frame_tiles, count):
    union = functools.reduce(lambda left, right: left | right, masks)
    seen = jnp.int32(0)
    picked = [[] for _ in range(count)]
    for tile in range(frame_tiles):
        bit = (union >> tile) & 1
        for spot in range(count):
            picked[spot].append((bit == 1) & (seen == spot))
        seen = seen + bit
    return picked


def forward_relayed(chunk, chunks, share, slabs):
    return ((chunk + 1) * share) // slabs > (chunk * share) // slabs


def backward_relayed(chunk, chunks, share, slabs):
    return chunk < (chunks * share + slabs - 1) // slabs


RELAYED = (forward_relayed, backward_relayed)


def cuts(chunks, first):
    spans, start, size = [], 0, first
    while start < chunks:
        stop = min(chunks, start + size)
        spans.append((start, stop))
        start, size = stop, size + 1
    return spans


def fused_kernel(
    group, slabs, count, chunks, tiles, counts, q_in, k_in, v_in, g_in,
    early, late,
    own, bias, outgoing, incoming, relay, parts, sums, result,
    send, recv, near, edge_send, edge_recv, relay_send, relay_recv,
    out_send, out_recv, out_near,
):
    place, slab = lax.axis_index("ulysses"), lax.axis_index("tm")
    side, member = place // group, place % group
    base = side * group
    frames = slabs * FRAMES_SLAB
    frame = slab * FRAMES_SLAB + side
    rows, frame_rows, width = q_in.shape[0], own.shape[1], own.shape[2]
    chunk_width = width // chunks
    edge = count * TILE
    frame_tiles = frame_rows // TILE

    turn = 2 * side - 1
    far_slab, onward_slab = slab + turn, slab - turn
    has_far = (far_slab >= 0) & (far_slab < slabs)
    has_onward = (onward_slab >= 0) & (onward_slab < slabs)
    across = {"ulysses": (1 - side) * group + member}
    far = {**across, "tm": jnp.clip(far_slab, 0, slabs - 1)}
    onward = {"tm": jnp.clip(onward_slab, 0, slabs - 1)}
    behind = {"tm": jnp.clip(far_slab, 0, slabs - 1)}
    from_end, from_start = slabs - 1 - slab, slab
    my_share = jnp.where(side == 1, from_end, from_start)
    other_share = jnp.where(side == 1, from_start, from_end)

    def lanes_of(which, start, size):
        return pl.ds(pl.multiple_of(which * width + start, LANES), size)

    def rows_of(which):
        return pl.ds(pl.multiple_of(which * rows, TILE), rows)

    sources = (k_in, v_in, q_in, g_in)
    pieces = {}
    key_cuts, query_cuts = cuts(chunks, 1), cuts(chunks, max(1, chunks // 2))

    def take(number, index, span):
        start, size = span[0] * chunk_width, (span[1] - span[0]) * chunk_width
        copy = pltpu.make_async_copy(
            sources[number].at[:, lanes_of(member, start, size)],
            own.at[number, rows_of(member), pl.ds(start, size)], near.at[number, index],
        )
        copy.start()
        pieces[number, index] = [copy]

    def trade(number, index, span):
        start, size = span[0] * chunk_width, (span[1] - span[0]) * chunk_width
        for step in range(1, group):
            peer = (member + step) % group
            copy = remote(
                sources[number].at[:, lanes_of(peer, start, size)],
                own.at[number, rows_of(member), pl.ds(start, size)],
                send.at[number, index, step - 1], recv.at[number, index, step - 1],
                {"ulysses": base + peer},
            )
            copy.start()
            pieces[number, index].append(copy)

    for index, span in enumerate(key_cuts):
        for number in (0, 1):
            take(number, index, span)

    barrier = pltpu.get_barrier_semaphore()

    def hail(device):
        pl.semaphore_signal(barrier, inc=1, device_id=device, device_id_type=MESH)

    for step in range(1, group):
        hail({"ulysses": base + (member + step) % group})
    hail(across)

    @pl.when(has_far)
    def _():
        hail(far)
        hail(behind)

    @pl.when(has_onward)
    def _():
        hail(onward)

    across_frame, far_frame = frame - turn, frame + turn
    picks = [
        nth_tiles(listing(tiles, counts, reader, frame, frame_tiles, frames), frame_tiles, count)
        for reader in (across_frame, far_frame)
    ]
    pl.semaphore_wait(
        barrier, group + jnp.where(has_far, 2, 0) + jnp.where(has_onward, 1, 0)
    )
    for index, span in enumerate(key_cuts):
        for number in (0, 1):
            trade(number, index, span)

    def edge_copy(phase, way, chunk, device):
        return remote(
            outgoing.at[phase, way, chunk], incoming.at[phase, way, chunk],
            edge_send.at[phase, way, chunk], edge_recv.at[phase, way, chunk], device,
        )

    def relay_in(phase, chunk):
        return remote(
            outgoing.at[phase, 1, chunk], relay.at[phase, chunk],
            edge_send.at[phase, 1, chunk], relay_recv.at[phase, chunk], across,
        )

    def relay_out(phase, chunk):
        return remote(
            relay.at[phase, chunk], incoming.at[phase, 1, chunk],
            relay_send.at[phase, chunk], edge_recv.at[phase, 1, chunk], onward,
        )

    def passes(phase, chunk):
        return has_onward & RELAYED[phase](chunk, chunks, other_share, slabs)

    def send_edges(phase, chunk):
        edge_copy(phase, 0, chunk, across).start()
        relayed = RELAYED[phase](chunk, chunks, my_share, slabs)

        @pl.when(has_far & jnp.logical_not(relayed))
        def _():
            edge_copy(phase, 1, chunk, far).start()

        @pl.when(has_far & relayed)
        def _():
            relay_in(phase, chunk).start()

    def pass_on(phase, chunk):
        @pl.when(passes(phase, chunk))
        def _():
            relay_in(phase, chunk).wait_recv()
            relay_out(phase, chunk).start()

    def receive_edges(phase, chunk):
        edge_copy(phase, 0, chunk, across).wait_recv()

        @pl.when(has_far)
        def _():
            edge_copy(phase, 1, chunk, far).wait_recv()

    def settle_edges(phase, chunk):
        edge_copy(phase, 0, chunk, across).wait_send()

        @pl.when(has_far)
        def _():
            edge_copy(phase, 1, chunk, far).wait_send()

        @pl.when(passes(phase, chunk))
        def _():
            relay_out(phase, chunk).wait_send()

    for index, span in enumerate(key_cuts):
        for number in (0, 1):
            for copy in pieces[number, index]:
                copy.wait()
        for chunk in range(*span):
            columns = pl.ds(chunk * chunk_width, chunk_width)
            for number in (0, 1):
                for way in range(2):
                    for spot in range(count):
                        chosen = own[number, pl.ds(0, TILE), columns]
                        for tile in range(1, frame_tiles):
                            here = own[number, pl.ds(tile * TILE, TILE), columns]
                            chosen = jnp.where(picks[way][spot][tile], here, chosen)
                        outgoing[0, way, chunk, number, pl.ds(spot * TILE, TILE)] = chosen
            send_edges(0, chunk)
        if index == 0:
            for piece, part in enumerate(query_cuts):
                for number in (2, 3):
                    take(number, piece, part)
                    trade(number, piece, part)

    @pl.when(jnp.logical_not(has_far))
    def _():
        for phase in range(2):
            for chunk in range(chunks):
                incoming[phase, 1, chunk] = jnp.zeros((2, edge, chunk_width), BF16)

    blocks, step_rows = bias.shape[0], bias.shape[2]
    across_rows = listing(tiles, counts, frame, across_frame, frame_tiles, frames)
    own_masks = listing(tiles, counts, frame, frame, frame_tiles, frames)
    far_rows = listing(tiles, counts, frame, far_frame, frame_tiles, frames)

    def edge_hits(masks):
        picked = nth_tiles(masks, frame_tiles, count)
        hits = []
        for spot in range(count):
            bit = jnp.int32(0)
            for tile in range(frame_tiles):
                bit = bit + jnp.where(picked[spot][tile], 1 << tile, 0)
            hits.append([(mask & bit) != 0 for mask in masks])
        return hits

    hits = edge_hits(across_rows)
    hits += [[((mask >> tile) & 1) == 1 for mask in own_masks] for tile in range(frame_tiles)]
    hits += edge_hits(far_rows)
    block_tiles = step_rows // TILE
    inner = lax.broadcasted_iota(jnp.int32, (1, step_rows), 1) // TILE
    for number, row in enumerate(hits):
        for block in range(blocks):
            line = jnp.full((1, step_rows), DEAD, F32)
            for spot in range(block_tiles):
                level = jnp.where(row[block * block_tiles + spot], 0.0, DEAD)
                line = jnp.where(inner == spot, level, line)
            bias[block, pl.ds(number, 1)] = line

    leaving = {}

    def share(phase, chunk):
        start = chunk * chunk_width
        target, columns = (early, late)[phase], pl.ds(start, chunk_width)
        there = lanes_of(member, start, chunk_width)
        copies = [pltpu.make_async_copy(
            result.at[phase, :, rows_of(member), columns], target.at[:, :, there],
            out_near.at[phase, chunk],
        )]
        for step in range(1, group):
            peer = (member + step) % group
            copies.append(remote(
                result.at[phase, :, rows_of(peer), columns], target.at[:, :, there],
                out_send.at[phase, chunk, step - 1], out_recv.at[phase, chunk, step - 1],
                {"ulysses": base + peer},
            ))
        for copy in copies:
            copy.start()
        leaving[phase, chunk] = copies

    def attend(chunk):
        @pl.loop(0, chunk_width // LANES)
        def _(pair):
            inside = pl.ds(pl.multiple_of(pair * LANES, LANES), LANES)
            lanes = pl.ds(pl.multiple_of(chunk * chunk_width + pair * LANES, LANES), LANES)

            def stacked(number):
                return jnp.concatenate([
                    incoming[0, 0, chunk, number, :, inside], own[number, :, lanes],
                    incoming[0, 1, chunk, number, :, inside],
                ])

            for block in range(blocks):
                span = pl.ds(block * step_rows, step_rows)
                out, grad_rows, key_part, value_part = heads_math(
                    own[2, span, lanes], own[3, span, lanes], stacked(0), stacked(1), bias[block],
                )
                result[0, 0, span, lanes] = out
                result[0, 1, span, lanes] = grad_rows
                for number, part in enumerate((key_part, value_part)):
                    if block:
                        part = part + sums[number]
                    if block + 1 < blocks:
                        sums[number] = part
                        continue
                    outgoing[1, 0, chunk, number, :, inside] = part[:edge].astype(BF16)
                    parts[number, :, lanes] = part[edge : edge + frame_rows]
                    outgoing[1, 1, chunk, number, :, inside] = part[edge + frame_rows :].astype(BF16)

    for chunk in range(chunks + LAG):
        if chunk < chunks:
            pass_on(0, chunk)
        ready = chunk - LAG
        if ready < 0:
            continue
        for piece, part in enumerate(query_cuts):
            if part[0] == ready:
                for number in (2, 3):
                    for copy in pieces[number, piece]:
                        copy.wait()
        receive_edges(0, ready)
        attend(ready)
        send_edges(1, ready)
        share(0, ready)

    for chunk in range(chunks):
        settle_edges(0, chunk)

    def gather(chunk):
        columns = pl.ds(chunk * chunk_width, chunk_width)
        for number in range(2):
            for tile in range(frame_tiles):
                span = pl.ds(tile * TILE, TILE)
                total = parts[number, span, columns]
                for way in range(2):
                    for spot in range(count):
                        part = incoming[1, way, chunk, number, pl.ds(spot * TILE, TILE)].astype(F32)
                        total = total + jnp.where(picks[way][spot][tile], part, 0.0)
                result[1, number, span, columns] = total.astype(BF16)
        share(1, chunk)

    for chunk in range(chunks + LAG):
        if chunk < chunks:
            pass_on(1, chunk)
        ready = chunk - LAG
        if ready < 0:
            continue
        for copy in leaving.pop((0, ready)):
            copy.wait()
        receive_edges(1, ready)
        gather(ready)

    for chunk in range(chunks):
        settle_edges(1, chunk)
        for copy in leaving.pop((1, chunk)):
            copy.wait()


def flush_kernel(early, late, *refs):
    sems = refs[4]
    copies = [
        pltpu.make_async_copy((early, late)[n // 2].at[n % 2], refs[n], sems.at[n])
        for n in range(4)
    ]
    for copy in copies:
        copy.start()
    for copy in copies:
        copy.wait()


def per_device(slabs, group, queries, key_vectors, value_vectors, grad_out, key_tiles, tile_counts):
    rows, columns = queries.shape
    width = columns // group
    frame_rows = rows * group
    frame_tiles = frame_rows // TILE
    count = max(1, frame_tiles // 8)
    edge = count * TILE
    ext_rows = frame_rows + 2 * edge
    chunk_width = LANES if width % CHUNK else CHUNK
    chunks = width // chunk_width
    step_rows = block_rows(frame_rows, ext_rows)
    blocks = frame_rows // step_rows
    key_pieces, query_pieces = len(cuts(chunks, 1)), len(cuts(chunks, max(1, chunks // 2)))
    most = max(key_pieces, query_pieces)

    smem = pl.BlockSpec(memory_space=pltpu.SMEM)
    vmem = pl.BlockSpec(memory_space=pltpu.VMEM)
    hbm = pl.BlockSpec(memory_space=pltpu.HBM)
    dma = pltpu.SemaphoreType.DMA
    arguments = [
        pltpu.with_memory_space_constraint(value, pltpu.HBM)
        for value in (key_tiles.T, tile_counts, queries, key_vectors, value_vectors, grad_out)
    ]
    results = pl.pallas_call(
        functools.partial(fused_kernel, group, slabs, count, chunks),
        out_shape=(jax.ShapeDtypeStruct((2, rows, columns), BF16),) * 2,
        in_specs=[smem, smem] + [hbm] * 4,
        out_specs=(vmem,) * 2,
        scratch_shapes=[
            pltpu.VMEM((4, frame_rows, width), BF16),
            pltpu.VMEM((blocks, ext_rows // TILE, step_rows), F32),
            pltpu.VMEM((2, 2, chunks, 2, edge, chunk_width), BF16),
            pltpu.VMEM((2, 2, chunks, 2, edge, chunk_width), BF16),
            pltpu.VMEM((2, chunks, 2, edge, chunk_width), BF16),
            pltpu.VMEM((2, frame_rows, width), F32),
            pltpu.VMEM((2, ext_rows if blocks > 1 else TILE, LANES), F32),
            pltpu.VMEM((2, 2, frame_rows, width), BF16),
            dma((4, most, group - 1)), dma((4, most, group - 1)), dma((4, most)),
            dma((2, 2, chunks)), dma((2, 2, chunks)), dma((2, chunks)), dma((2, chunks)),
            dma((2, chunks, group - 1)), dma((2, chunks, group - 1)), dma((2, chunks)),
        ],
        compiler_params=pltpu.CompilerParams(
            collective_id=0, has_side_effects=True, vmem_limit_bytes=32 << 20
        ),
        name="frame_attention",
    )(*arguments)
    return pl.pallas_call(
        flush_kernel,
        out_shape=(jax.ShapeDtypeStruct((rows, columns), BF16),) * 4,
        in_specs=[vmem] * 2,
        out_specs=(hbm,) * 4,
        scratch_shapes=[dma((4,))],
        compiler_params=pltpu.CompilerParams(vmem_limit_bytes=16 << 20),
        name="flush_results",
    )(*results)


def solution(mesh):
    tokens = P(("clips", "tm", "ulysses"), None)
    group = mesh.shape["ulysses"] // FRAMES_SLAB
    return jax.shard_map(
        functools.partial(per_device, mesh.shape["tm"], group),
        mesh=mesh,
        in_specs=(tokens, tokens, tokens, tokens, P("clips", None), P("clips")),
        out_specs=(tokens,) * 4,
        check_vma=False,
    )
```

time: 45.6 us -> 43.1 us (0.945)
  Pallas kernels: 44.8 us -> 42.2 us
    pallas_call x2, Pallas kernels: 44.8 us -> 42.2 us  [the longest x1 40.5 us: per_device(): pl.pallas_call(functools.partial(fused_kernel, group, slabs, count, chunk...]
where the time goes in v2:
time: 43.1 us; the launch traced here: 42.9 us
  Pallas kernels  42.2 us (98%)
  between operations  0.64 us (1%)
    pallas_call x1, Pallas kernels, per_device(): pl.pallas_call(functools.partial(fused_kernel, group, slabs, count, chunk...  40.5 us
    pallas_call x1, Pallas kernels, per_device(): pl.pallas_call(flush_kernel, out_shape=(jax.ShapeDtypeStruct((rows, colum...  1.69 us

profile of v2, /device:TPU:9, one launch (start us, length us, event | category | flops | bytes accessed | tf_op | source)
XLA Modules:
  0.0 42.9 jit_solution(7961392936080790254)
XLA Ops:
  0.6 40.5 %frame_attention.1 = (bf16[2,128,3072]{2,1,0:T(8,128)(2,1)S(1)}, bf16[2,128,3072]{2,1,0:T(8,128)(2,1)S(1)}) custom-call(s32[3,32]{1,0:T(4,128)} %bitcast.1, s32[32]{0:T(128)} %counts.1, bf16[128,3072]{1,0:T(8,128)(2,1)} %q_in.1, bf16[128,3072]{1,0:T(8,128)(2,1)} %k_in.1, bf16[128,3072]{1,0:T(8,128)(2,1)} %v_in.1, bf16[128,3072]{1,0:T(8,128)(2,1)} %g_in.1), custom_call_target="tpu_custom_call" | custom-call | tf_op jit(solution)/shard_map/frame_attention/pallas_call | solution.py:459
  41.2 1.7 %flush_results.1 = (bf16[128,3072]{1,0:T(8,128)(2,1)}, bf16[128,3072]{1,0:T(8,128)(2,1)}, bf16[128,3072]{1,0:T(8,128)(2,1)}, bf16[128,3072]{1,0:T(8,128)(2,1)}) custom-call(bf16[2,128,3072]{2,1,0:T(8,128)(2,1)S(1)} %get-tuple-element.6.early, bf16[2,128,3072]{2,1,0:T(8,128)(2,1)S(1)} %get-tuple-element.7.late), custom_call_target="tpu_custom_call" | custom-call | tf_op jit(solution)/shard_map/flush_results/pallas_call | solution.py:482

commit v3 on v2

--- a/solution.py
+++ b/solution.py
@@ -15,6 +15,7 @@
 BLOCK_LIMIT = 384 * 512
 CHUNK = 256
 LAG = 1
+HOLD = 1
 MESH = pl.DeviceIdType.MESH
 BF16 = jnp.bfloat16
 F32 = jnp.float32
@@ -95,15 +96,21 @@
     return picked
 
 
-def forward_relayed(chunk, chunks, share, slabs):
-    return ((chunk + 1) * share) // slabs > (chunk * share) // slabs
-
-
-def backward_relayed(chunk, chunks, share, slabs):
-    return chunk < (chunks * share + slabs - 1) // slabs
-
-
-RELAYED = (forward_relayed, backward_relayed)
+def chunk_spans(width):
+    sizes = [LANES] * (width // LANES)
+    if width % CHUNK == 0 and width > CHUNK:
+        sizes = [LANES] + [CHUNK] * (width // CHUNK - 1) + [CHUNK - LANES]
+    return [(sum(sizes[:n]), size) for n, size in enumerate(sizes)]
+
+
+def relayed(phase, chunk, share, slabs, spans):
+    if phase == 0 and chunk + 1 == len(spans):
+        return share < 0
+    if phase == 0:
+        return ((chunk + 1) * share) // slabs > (chunk * share) // slabs
+    start, size = spans[chunk]
+    total = spans[-1][0] + spans[-1][1]
+    return (start + size) * slabs <= total * share
 
 
 def cuts(chunks, first):
@@ -116,11 +123,11 @@
 
 
 def fused_kernel(
-    group, slabs, count, chunks, tiles, counts, q_in, k_in, v_in, g_in,
+    group, slabs, count, spans, tiles_in, counts_in, q_in, k_in, v_in, g_in,
     early, late,
     own, bias, outgoing, incoming, relay, parts, sums, result,
     send, recv, near, edge_send, edge_recv, relay_send, relay_recv,
-    out_send, out_recv, out_near,
+    out_send, out_recv, out_near, tiles, counts, list_sem,
 ):
     place, slab = lax.axis_index("ulysses"), lax.axis_index("tm")
     side, member = place // group, place % group
@@ -128,7 +135,7 @@
     frames = slabs * FRAMES_SLAB
     frame = slab * FRAMES_SLAB + side
     rows, frame_rows, width = q_in.shape[0], own.shape[1], own.shape[2]
-    chunk_width = width // chunks
+    chunks, widest = len(spans), outgoing.shape[5]
     edge = count * TILE
     frame_tiles = frame_rows // TILE
 
@@ -155,7 +162,8 @@
     key_cuts, query_cuts = cuts(chunks, 1), cuts(chunks, max(1, chunks // 2))
 
     def take(number, index, span):
-        start, size = span[0] * chunk_width, (span[1] - span[0]) * chunk_width
+        start = spans[span[0]][0]
+        size = sum(spans[span[1] - 1]) - start
         copy = pltpu.make_async_copy(
             sources[number].at[:, lanes_of(member, start, size)],
             own.at[number, rows_of(member), pl.ds(start, size)], near.at[number, index],
@@ -164,7 +172,8 @@
         pieces[number, index] = [copy]
 
     def trade(number, index, span):
-        start, size = span[0] * chunk_width, (span[1] - span[0]) * chunk_width
+        start = spans[span[0]][0]
+        size = sum(spans[span[1] - 1]) - start
         for step in range(1, group):
             peer = (member + step) % group
             copy = remote(
@@ -176,10 +185,6 @@
             copy.start()
             pieces[number, index].append(copy)
 
-    for index, span in enumerate(key_cuts):
-        for number in (0, 1):
-            take(number, index, span)
-
     barrier = pltpu.get_barrier_semaphore()
 
     def hail(device):
@@ -198,6 +203,18 @@
     def _():
         hail(onward)
 
+    lists = [
+        pltpu.make_async_copy(tiles_in, tiles, list_sem.at[0]),
+        pltpu.make_async_copy(counts_in, counts, list_sem.at[1]),
+    ]
+    for copy in lists:
+        copy.start()
+    for index, span in enumerate(key_cuts):
+        for number in (0, 1):
+            take(number, index, span)
+
+    for copy in lists:
+        copy.wait()
     across_frame, far_frame = frame - turn, frame + turn
     picks = [
         nth_tiles(listing(tiles, counts, reader, frame, frame_tiles, frames), frame_tiles, count)
@@ -210,36 +227,41 @@
         for number in (0, 1):
             trade(number, index, span)
 
+    def lot(ref, chunk):
+        return ref if spans[chunk][1] == widest else ref.at[:, :, pl.ds(0, spans[chunk][1])]
+
     def edge_copy(phase, way, chunk, device):
         return remote(
-            outgoing.at[phase, way, chunk], incoming.at[phase, way, chunk],
+            lot(outgoing.at[phase, way, chunk], chunk), lot(incoming.at[phase, way, chunk], chunk),
             edge_send.at[phase, way, chunk], edge_recv.at[phase, way, chunk], device,
         )
 
     def relay_in(phase, chunk):
         return remote(
-            outgoing.at[phase, 1, chunk], relay.at[phase, chunk],
+            lot(outgoing.at[phase, 1, chunk], chunk), lot(relay.at[phase, chunk], chunk),
             edge_send.at[phase, 1, chunk], relay_recv.at[phase, chunk], across,
         )
 
     def relay_out(phase, chunk):
         return remote(
-            relay.at[phase, chunk], incoming.at[phase, 1, chunk],
+            lot(relay.at[phase, chunk], chunk), lot(incoming.at[phase, 1, chunk], chunk),
             relay_send.at[phase, chunk], edge_recv.at[phase, 1, chunk], onward,
         )
 
     def passes(phase, chunk):
-        return has_onward & RELAYED[phase](chunk, chunks, other_share, slabs)
-
-    def send_edges(phase, chunk):
+        return has_onward & relayed(phase, chunk, other_share, slabs, spans)
+
+    def send_across(phase, chunk):
         edge_copy(phase, 0, chunk, across).start()
-        relayed = RELAYED[phase](chunk, chunks, my_share, slabs)
-
-        @pl.when(has_far & jnp.logical_not(relayed))
+
+    def send_far(phase, chunk):
+        around = relayed(phase, chunk, my_share, slabs, spans)
+
+        @pl.when(has_far & jnp.logical_not(around))
         def _():
             edge_copy(phase, 1, chunk, far).start()
 
-        @pl.when(has_far & relayed)
+        @pl.when(has_far & around)
         def _():
             relay_in(phase, chunk).start()
 
@@ -272,7 +294,8 @@
             for copy in pieces[number, index]:
                 copy.wait()
         for chunk in range(*span):
-            columns = pl.ds(chunk * chunk_width, chunk_width)
+            columns = pl.ds(*spans[chunk])
+            size = spans[chunk][1]
             for number in (0, 1):
                 for way in range(2):
                     for spot in range(count):
@@ -280,8 +303,9 @@
                         for tile in range(1, frame_tiles):
                             here = own[number, pl.ds(tile * TILE, TILE), columns]
                             chosen = jnp.where(picks[way][spot][tile], here, chosen)
-                        outgoing[0, way, chunk, number, pl.ds(spot * TILE, TILE)] = chosen
-            send_edges(0, chunk)
+                        outgoing[0, way, chunk, number, pl.ds(spot * TILE, TILE), pl.ds(0, size)] = chosen
+            send_far(0, chunk)
+            send_across(0, chunk)
         if index == 0:
             for piece, part in enumerate(query_cuts):
                 for number in (2, 3):
@@ -292,7 +316,7 @@
     def _():
         for phase in range(2):
             for chunk in range(chunks):
-                incoming[phase, 1, chunk] = jnp.zeros((2, edge, chunk_width), BF16)
+                incoming[phase, 1, chunk] = jnp.zeros((2, edge, widest), BF16)
 
     blocks, step_rows = bias.shape[0], bias.shape[2]
     across_rows = listing(tiles, counts, frame, across_frame, frame_tiles, frames)
@@ -325,9 +349,9 @@
     leaving = {}
 
     def share(phase, chunk):
-        start = chunk * chunk_width
-        target, columns = (early, late)[phase], pl.ds(start, chunk_width)
-        there = lanes_of(member, start, chunk_width)
+        start, size = spans[chunk]
+        target, columns = (early, late)[phase], pl.ds(start, size)
+        there = lanes_of(member, start, size)
         copies = [pltpu.make_async_copy(
             result.at[phase, :, rows_of(member), columns], target.at[:, :, there],
             out_near.at[phase, chunk],
@@ -344,10 +368,10 @@
         leaving[phase, chunk] = copies
 
     def attend(chunk):
-        @pl.loop(0, chunk_width // LANES)
+        @pl.loop(0, spans[chunk][1] // LANES)
         def _(pair):
             inside = pl.ds(pl.multiple_of(pair * LANES, LANES), LANES)
-            lanes = pl.ds(pl.multiple_of(chunk * chunk_width + pair * LANES, LANES), LANES)
+            lanes = pl.ds(pl.multiple_of(spans[chunk][0] + pair * LANES, LANES), LANES)
 
             def stacked(number):
                 return jnp.concatenate([
@@ -385,22 +409,26 @@
                         copy.wait()
         receive_edges(0, ready)
         attend(ready)
-        send_edges(1, ready)
+        send_far(1, ready)
+        if ready >= HOLD:
+            send_across(1, ready - HOLD)
         share(0, ready)
 
+    for chunk in range(max(0, chunks - HOLD), chunks):
+        send_across(1, chunk)
     for chunk in range(chunks):
         settle_edges(0, chunk)
 
     def gather(chunk):
-        columns = pl.ds(chunk * chunk_width, chunk_width)
+        columns, size = pl.ds(*spans[chunk]), spans[chunk][1]
         for number in range(2):
             for tile in range(frame_tiles):
                 span = pl.ds(tile * TILE, TILE)
                 total = parts[number, span, columns]
                 for way in range(2):
                     for spot in range(count):
-                        part = incoming[1, way, chunk, number, pl.ds(spot * TILE, TILE)].astype(F32)
-                        total = total + jnp.where(picks[way][spot][tile], part, 0.0)
+                        part = incoming[1, way, chunk, number, pl.ds(spot * TILE, TILE), pl.ds(0, size)]
+                        total = total + jnp.where(picks[way][spot][tile], part.astype(F32), 0.0)
                 result[1, number, span, columns] = total.astype(BF16)
         share(1, chunk)
 
@@ -441,14 +469,13 @@
     count = max(1, frame_tiles // 8)
     edge = count * TILE
     ext_rows = frame_rows + 2 * edge
-    chunk_width = LANES if width % CHUNK else CHUNK
-    chunks = width // chunk_width
+    spans = chunk_spans(width)
+    chunks, chunk_width = len(spans), max(size for _, size in spans)
     step_rows = block_rows(frame_rows, ext_rows)
     blocks = frame_rows // step_rows
     key_pieces, query_pieces = len(cuts(chunks, 1)), len(cuts(chunks, max(1, chunks // 2)))
     most = max(key_pieces, query_pieces)
 
-    smem = pl.BlockSpec(memory_space=pltpu.SMEM)
     vmem = pl.BlockSpec(memory_space=pltpu.VMEM)
     hbm = pl.BlockSpec(memory_space=pltpu.HBM)
     dma = pltpu.SemaphoreType.DMA
@@ -457,9 +484,9 @@
         for value in (key_tiles.T, tile_counts, queries, key_vectors, value_vectors, grad_out)
     ]
     results = pl.pallas_call(
-        functools.partial(fused_kernel, group, slabs, count, chunks),
+        functools.partial(fused_kernel, group, slabs, count, spans),
         out_shape=(jax.ShapeDtypeStruct((2, rows, columns), BF16),) * 2,
-        in_specs=[smem, smem] + [hbm] * 4,
+        in_specs=[hbm] * 6,
         out_specs=(vmem,) * 2,
         scratch_shapes=[
             pltpu.VMEM((4, frame_rows, width), BF16),
@@ -473,6 +500,7 @@
             dma((4, most, group - 1)), dma((4, most, group - 1)), dma((4, most)),
             dma((2, 2, chunks)), dma((2, 2, chunks)), dma((2, chunks)), dma((2, chunks)),
             dma((2, chunks, group - 1)), dma((2, chunks, group - 1)), dma((2, chunks)),
+            pltpu.SMEM(key_tiles.T.shape, jnp.int32), pltpu.SMEM(tile_counts.shape, jnp.int32), dma((2,)),
         ],
         compiler_params=pltpu.CompilerParams(
             collective_id=0, has_side_effects=True, vmem_limit_bytes=32 << 20

time: 43.1 us -> 40.8 us (0.947)
  Pallas kernels: 42.2 us -> 39.7 us
    pallas_call x1, Pallas kernels: 40.5 us -> 38 us  [per_device(): pl.pallas_call(functools.partial(fused_kernel, group, slabs, count, spans...]
where the time goes in v3:
time: 40.8 us; the launch traced here: 40.3 us
  Pallas kernels  39.7 us (97%)
  between operations  0.64 us (2%)
    pallas_call x1, Pallas kernels, per_device(): pl.pallas_call(functools.partial(fused_kernel, group, slabs, count, spans...  38 us
    pallas_call x1, Pallas kernels, per_device(): pl.pallas_call(flush_kernel, out_shape=(jax.ShapeDtypeStruct((rows, colum...  1.69 us

profile of v3, /device:TPU:9, one launch (start us, length us, event | category | flops | bytes accessed | tf_op | source)
XLA Modules:
  0.0 40.3 jit_solution(5925378620110475954)
XLA Ops:
  0.6 38.0 %frame_attention.1 = (bf16[2,128,3072]{2,1,0:T(8,128)(2,1)S(1)}, bf16[2,128,3072]{2,1,0:T(8,128)(2,1)S(1)}) custom-call(s32[3,32]{1,0:T(4,128)} %bitcast.1, s32[32]{0:T(128)} %counts_in.1, bf16[128,3072]{1,0:T(8,128)(2,1)} %q_in.1, bf16[128,3072]{1,0:T(8,128)(2,1)} %k_in.1, bf16[128,3072]{1,0:T(8,128)(2,1)} %v_in.1, bf16[128,3072]{1,0:T(8,128)(2,1)} %g_in.1), custom_call_target="tpu_custom_call" | custom-call | tf_op jit(solution)/shard_map/frame_attention/pallas_call | solution.py:486
  38.6 1.7 %flush_results.1 = (bf16[128,3072]{1,0:T(8,128)(2,1)}, bf16[128,3072]{1,0:T(8,128)(2,1)}, bf16[128,3072]{1,0:T(8,128)(2,1)}, bf16[128,3072]{1,0:T(8,128)(2,1)}) custom-call(bf16[2,128,3072]{2,1,0:T(8,128)(2,1)S(1)} %get-tuple-element.6.early, bf16[2,128,3072]{2,1,0:T(8,128)(2,1)S(1)} %get-tuple-element.7.late), custom_call_target="tpu_custom_call" | custom-call | tf_op jit(solution)/shard_map/flush_results/pallas_call | solution.py:510

commit v4 on v3

--- a/solution.py
+++ b/solution.py
@@ -127,7 +127,8 @@
     early, late,
     own, bias, outgoing, incoming, relay, parts, sums, result,
     send, recv, near, edge_send, edge_recv, relay_send, relay_recv,
-    out_send, out_recv, out_near, tiles, counts, list_sem,
+    out_send, out_recv, out_near, tiles, counts, list_sem, lead, lead_sem, offer, offered,
+    offer_send, offer_recv,
 ):
     place, slab = lax.axis_index("ulysses"), lax.axis_index("tm")
     side, member = place // group, place % group
@@ -158,7 +159,14 @@
         return pl.ds(pl.multiple_of(which * rows, TILE), rows)
 
     sources = (k_in, v_in, q_in, g_in)
-    pieces = {}
+    pieces, nearby, sent = {}, {}, []
+
+    def arrive(number, index):
+        for copy in nearby.pop((number, index), []):
+            copy.wait()
+        for copy in pieces[number, index]:
+            copy.wait_recv()
+
     key_cuts, query_cuts = cuts(chunks, 1), cuts(chunks, max(1, chunks // 2))
 
     def take(number, index, span):
@@ -169,30 +177,38 @@
             own.at[number, rows_of(member), pl.ds(start, size)], near.at[number, index],
         )
         copy.start()
-        pieces[number, index] = [copy]
+        nearby[number, index], pieces[number, index] = [copy], []
 
     def trade(number, index, span):
         start = spans[span[0]][0]
         size = sum(spans[span[1] - 1]) - start
         for step in range(1, group):
             peer = (member + step) % group
+            source = sources[number].at[:, lanes_of(peer, start, size)]
+            if number < 2 and index == 0:
+                source = lead.at[number, step - 1]
             copy = remote(
-                sources[number].at[:, lanes_of(peer, start, size)],
-                own.at[number, rows_of(member), pl.ds(start, size)],
+                source, own.at[number, rows_of(member), pl.ds(start, size)],
                 send.at[number, index, step - 1], recv.at[number, index, step - 1],
                 {"ulysses": base + peer},
             )
             copy.start()
             pieces[number, index].append(copy)
+            sent.append(copy)
 
     barrier = pltpu.get_barrier_semaphore()
+    eager, own_tiles = group == FRAMES_SLAB, rows // TILE
+
+    def opposite(step):
+        return {"ulysses": (1 - side) * group + (member + step) % group}
 
     def hail(device):
         pl.semaphore_signal(barrier, inc=1, device_id=device, device_id_type=MESH)
 
     for step in range(1, group):
         hail({"ulysses": base + (member + step) % group})
-    hail(across)
+    for step in range(group if eager else 1):
+        hail(opposite(step))
 
     @pl.when(has_far)
     def _():
@@ -209,6 +225,16 @@
     ]
     for copy in lists:
         copy.start()
+    leads = []
+    for number in (0, 1):
+        for step in range(1, group):
+            peer = (member + step) % group
+            copy = pltpu.make_async_copy(
+                sources[number].at[:, lanes_of(peer, 0, spans[0][1])],
+                lead.at[number, step - 1], lead_sem.at[number, step - 1],
+            )
+            copy.start()
+            leads.append(copy)
     for index, span in enumerate(key_cuts):
         for number in (0, 1):
             take(number, index, span)
@@ -220,12 +246,47 @@
         nth_tiles(listing(tiles, counts, reader, frame, frame_tiles, frames), frame_tiles, count)
         for reader in (across_frame, far_frame)
     ]
+    def offer_copy(step):
+        return remote(
+            offer.at[step], offered.at[step], offer_send.at[step], offer_recv.at[step],
+            opposite(step),
+        )
+
+    def any_of(flags):
+        return functools.reduce(lambda left, right: left | right, flags)
+
+    def candidate(step, number, inner):
+        start = inner * TILE
+        if step:
+            return lead[number, step - 1, pl.ds(start, TILE)]
+        place_rows = pl.ds(pl.multiple_of(member * rows + start, TILE), TILE)
+        return own[number, place_rows, pl.ds(0, spans[0][1])]
+
+    for copy in leads:
+        copy.wait()
+    if eager:
+        for number in (0, 1):
+            for copy in nearby.pop((number, 0)):
+                copy.wait()
+            for step in range(group):
+                for spot in range(count):
+                    chosen = candidate(step, number, 0)
+                    for inner in range(1, own_tiles):
+                        flag = any_of([
+                            (member == m) & picks[0][spot][m * own_tiles + inner]
+                            for m in range(group)
+                        ])
+                        chosen = jnp.where(flag, candidate(step, number, inner), chosen)
+                    offer[step, number, pl.ds(spot * TILE, TILE)] = chosen
     pl.semaphore_wait(
-        barrier, group + jnp.where(has_far, 2, 0) + jnp.where(has_onward, 1, 0)
+        barrier, (2 * group - 1 if eager else group) + jnp.where(has_far, 2, 0) + jnp.where(has_onward, 1, 0)
     )
     for index, span in enumerate(key_cuts):
         for number in (0, 1):
             trade(number, index, span)
+        if eager and index == 0:
+            for step in range(group):
+                offer_copy(step).start()
 
     def lot(ref, chunk):
         return ref if spans[chunk][1] == widest else ref.at[:, :, pl.ds(0, spans[chunk][1])]
@@ -252,6 +313,8 @@
         return has_onward & relayed(phase, chunk, other_share, slabs, spans)
 
     def send_across(phase, chunk):
+        if eager and (phase, chunk) == (0, 0):
+            return
         edge_copy(phase, 0, chunk, across).start()
 
     def send_far(phase, chunk):
@@ -271,15 +334,38 @@
             relay_in(phase, chunk).wait_recv()
             relay_out(phase, chunk).start()
 
+    def accept():
+        size = spans[0][1]
+        for step in range(group):
+            offer_copy(step).wait_recv()
+        for spot in range(count):
+            rows_here = pl.ds(spot * TILE, TILE)
+            for number in (0, 1):
+                chosen = offered[0, number, rows_here]
+                for step in range(1, group):
+                    flag = any_of([
+                        ((member - step + group) % group == tile // own_tiles) & across_picks[spot][tile]
+                        for tile in range(frame_tiles)
+                    ])
+                    chosen = jnp.where(flag, offered[step, number, rows_here], chosen)
+                incoming[0, 0, 0, number, rows_here, pl.ds(0, size)] = chosen
+
     def receive_edges(phase, chunk):
-        edge_copy(phase, 0, chunk, across).wait_recv()
+        if eager and (phase, chunk) == (0, 0):
+            accept()
+        else:
+            edge_copy(phase, 0, chunk, across).wait_recv()
 
         @pl.when(has_far)
         def _():
             edge_copy(phase, 1, chunk, far).wait_recv()
 
     def settle_edges(phase, chunk):
-        edge_copy(phase, 0, chunk, across).wait_send()
+        if eager and (phase, chunk) == (0, 0):
+            for step in range(group):
+                offer_copy(step).wait_send()
+        else:
+            edge_copy(phase, 0, chunk, across).wait_send()
 
         @pl.when(has_far)
         def _():
@@ -291,8 +377,7 @@
 
     for index, span in enumerate(key_cuts):
         for number in (0, 1):
-            for copy in pieces[number, index]:
-                copy.wait()
+            arrive(number, index)
         for chunk in range(*span):
             columns = pl.ds(*spans[chunk])
             size = spans[chunk][1]
@@ -320,6 +405,7 @@
 
     blocks, step_rows = bias.shape[0], bias.shape[2]
     across_rows = listing(tiles, counts, frame, across_frame, frame_tiles, frames)
+    across_picks = nth_tiles(across_rows, frame_tiles, count)
     own_masks = listing(tiles, counts, frame, frame, frame_tiles, frames)
     far_rows = listing(tiles, counts, frame, far_frame, frame_tiles, frames)
 
@@ -405,8 +491,7 @@
         for piece, part in enumerate(query_cuts):
             if part[0] == ready:
                 for number in (2, 3):
-                    for copy in pieces[number, piece]:
-                        copy.wait()
+                    arrive(number, piece)
         receive_edges(0, ready)
         attend(ready)
         send_far(1, ready)
@@ -416,6 +501,8 @@
 
     for chunk in range(max(0, chunks - HOLD), chunks):
         send_across(1, chunk)
+    for copy in sent:
+        copy.wait_send()
     for chunk in range(chunks):
         settle_edges(0, chunk)
 
@@ -440,12 +527,17 @@
             continue
         for copy in leaving.pop((0, ready)):
             copy.wait()
+        if ready:
+            settle_edges(1, ready - 1)
+        if ready > 1:
+            for copy in leaving.pop((1, ready - 2)):
+                copy.wait()
         receive_edges(1, ready)
         gather(ready)
 
-    for chunk in range(chunks):
-        settle_edges(1, chunk)
-        for copy in leaving.pop((1, chunk)):
+    settle_edges(1, chunks - 1)
+    for copies in leaving.values():
+        for copy in copies:
             copy.wait()
 
 
@@ -501,6 +593,9 @@
             dma((2, 2, chunks)), dma((2, 2, chunks)), dma((2, chunks)), dma((2, chunks)),
             dma((2, chunks, group - 1)), dma((2, chunks, group - 1)), dma((2, chunks)),
             pltpu.SMEM(key_tiles.T.shape, jnp.int32), pltpu.SMEM(tile_counts.shape, jnp.int32), dma((2,)),
+            pltpu.VMEM((2, group - 1, rows, spans[0][1]), BF16), dma((2, group - 1)),
+            pltpu.VMEM((group, 2, edge, spans[0][1]), BF16), pltpu.VMEM((group, 2, edge, spans[0][1]), BF16),
+            dma((group,)), dma((group,)),
         ],
         compiler_params=pltpu.CompilerParams(
             collective_id=0, has_side_effects=True, vmem_limit_bytes=32 << 20

time: 40.8 us -> 40.3 us (0.988)
  Pallas kernels: 39.7 us -> 39 us
    pallas_call x1, Pallas kernels: 38 us -> 37.4 us  [per_device(): pl.pallas_call(functools.partial(fused_kernel, group, slabs, count, spans...]
where the time goes in v4:
time: 40.3 us; the launch traced here: 39.7 us
  Pallas kernels  39 us (97%)
  between operations  0.64 us (2%)
    pallas_call x1, Pallas kernels, per_device(): pl.pallas_call(functools.partial(fused_kernel, group, slabs, count, spans...  37.4 us
    pallas_call x1, Pallas kernels, per_device(): pl.pallas_call(flush_kernel, out_shape=(jax.ShapeDtypeStruct((rows, colum...  1.69 us

profile of v4, /device:TPU:9, one launch (start us, length us, event | category | flops | bytes accessed | tf_op | source)
XLA Modules:
  0.0 39.7 jit_solution(3825047282228360147)
XLA Ops:
  0.6 37.4 %frame_attention.1 = (bf16[2,128,3072]{2,1,0:T(8,128)(2,1)S(1)}, bf16[2,128,3072]{2,1,0:T(8,128)(2,1)S(1)}) custom-call(s32[3,32]{1,0:T(4,128)} %bitcast.1, s32[32]{0:T(128)} %counts_in.1, bf16[128,3072]{1,0:T(8,128)(2,1)} %q_in.1, bf16[128,3072]{1,0:T(8,128)(2,1)} %k_in.1, bf16[128,3072]{1,0:T(8,128)(2,1)} %v_in.1, bf16[128,3072]{1,0:T(8,128)(2,1)} %g_in.1), custom_call_target="tpu_custom_call" | custom-call | tf_op jit(solution)/shard_map/frame_attention/pallas_call | solution.py:578
  38.0 1.7 %flush_results.1 = (bf16[128,3072]{1,0:T(8,128)(2,1)}, bf16[128,3072]{1,0:T(8,128)(2,1)}, bf16[128,3072]{1,0:T(8,128)(2,1)}, bf16[128,3072]{1,0:T(8,128)(2,1)}) custom-call(bf16[2,128,3072]{2,1,0:T(8,128)(2,1)S(1)} %get-tuple-element.6.early, bf16[2,128,3072]{2,1,0:T(8,128)(2,1)S(1)} %get-tuple-element.7.late), custom_call_target="tpu_custom_call" | custom-call | tf_op jit(solution)/shard_map/flush_results/pallas_call | solution.py:605

commit v5 on v4

--- a/solution.py
+++ b/solution.py
@@ -205,19 +205,19 @@
     def hail(device):
         pl.semaphore_signal(barrier, inc=1, device_id=device, device_id_type=MESH)
 
+    @pl.when(has_far)
+    def _():
+        hail(far)
+        hail(behind)
+
+    @pl.when(has_onward)
+    def _():
+        hail(onward)
+
     for step in range(1, group):
         hail({"ulysses": base + (member + step) % group})
     for step in range(group if eager else 1):
         hail(opposite(step))
-
-    @pl.when(has_far)
-    def _():
-        hail(far)
-        hail(behind)
-
-    @pl.when(has_onward)
-    def _():
-        hail(onward)
 
     lists = [
         pltpu.make_async_copy(tiles_in, tiles, list_sem.at[0]),
@@ -281,12 +281,14 @@
     pl.semaphore_wait(
         barrier, (2 * group - 1 if eager else group) + jnp.where(has_far, 2, 0) + jnp.where(has_onward, 1, 0)
     )
-    for index, span in enumerate(key_cuts):
+    if eager:
+        for step in range(group):
+            offer_copy(step).start()
+    for number in (0, 1):
+        trade(number, 0, key_cuts[0])
+    for index, span in enumerate(key_cuts[1:]):
         for number in (0, 1):
-            trade(number, index, span)
-        if eager and index == 0:
-            for step in range(group):
-                offer_copy(step).start()
+            trade(number, index + 1, span)
 
     def lot(ref, chunk):
         return ref if spans[chunk][1] == widest else ref.at[:, :, pl.ds(0, spans[chunk][1])]

time: 40.3 us -> 40.2 us (level)
  no operation moved by 1% of the time
where the time goes in v5:
time: 40.2 us; the launch traced here: 39.7 us
  Pallas kernels  39 us (97%)
  between operations  0.64 us (2%)
    pallas_call x1, Pallas kernels, per_device(): pl.pallas_call(functools.partial(fused_kernel, group, slabs, count, spans...  37.3 us
    pallas_call x1, Pallas kernels, per_device(): pl.pallas_call(flush_kernel, out_shape=(jax.ShapeDtypeStruct((rows, colum...  1.69 us

profile of v5, /device:TPU:9, one launch (start us, length us, event | category | flops | bytes accessed | tf_op | source)
XLA Modules:
  0.0 39.7 jit_solution(9776352486645420107)
XLA Ops:
  0.6 37.3 %frame_attention.1 = (bf16[2,128,3072]{2,1,0:T(8,128)(2,1)S(1)}, bf16[2,128,3072]{2,1,0:T(8,128)(2,1)S(1)}) custom-call(s32[3,32]{1,0:T(4,128)} %bitcast.1, s32[32]{0:T(128)} %counts_in.1, bf16[128,3072]{1,0:T(8,128)(2,1)} %q_in.1, bf16[128,3072]{1,0:T(8,128)(2,1)} %k_in.1, bf16[128,3072]{1,0:T(8,128)(2,1)} %v_in.1, bf16[128,3072]{1,0:T(8,128)(2,1)} %g_in.1), custom_call_target="tpu_custom_call" | custom-call | tf_op jit(solution)/shard_map/frame_attention/pallas_call | solution.py:580
  38.0 1.7 %flush_results.1 = (bf16[128,3072]{1,0:T(8,128)(2,1)}, bf16[128,3072]{1,0:T(8,128)(2,1)}, bf16[128,3072]{1,0:T(8,128)(2,1)}, bf16[128,3072]{1,0:T(8,128)(2,1)}) custom-call(bf16[2,128,3072]{2,1,0:T(8,128)(2,1)S(1)} %get-tuple-element.6.early, bf16[2,128,3072]{2,1,0:T(8,128)(2,1)S(1)} %get-tuple-element.7.late), custom_call_target="tpu_custom_call" | custom-call | tf_op jit(solution)/shard_map/flush_results/pallas_call | solution.py:607
